TPU v7x, 32 devices: a whole 2x2x4 slice. The times are simulated.
32 devices in a mesh: tp: 4 (over y, core), dp: 8 (over z, x).
Axes of the slice: x: 2, y: 2, z: 4, core: 2. Of those that a mesh axis runs over, the one named last changes fastest.
Arguments:
- tokens: bfloat16 [24, 1024, 768], P('dp', 'tp'), may hold values from -6 to 6
- lengths: int32 [24], P('dp'), may hold values from 196 to 1024, as said below
- ln_gain: float32 [768], replicated, may hold values from 0.1 to 1.9
- w_qkv: bfloat16 [768, 2304], P(None, 'tp'), may hold values from -0.21875 to 0.21875
- q_gain: float32 [12, 64], P('tp'), may hold values from 0.1 to 1.9
- k_gain: float32 [12, 64], P('tp'), may hold values from 0.1 to 1.9
- w_proj: bfloat16 [768, 768], P('tp'), may hold values from -1.75 to 1.75
- w_fc1: bfloat16 [768, 3072], P(None, 'tp'), may hold values from -0.21875 to 0.21875
- b_fc1: float32 [3072], P('tp'), may hold values from -3 to 3
- w_fc2: bfloat16 [3072, 768], P('tp'), may hold values from -0.109375 to 0.109375
- b_fc2: float32 [768], replicated, may hold values from -2 to 2
- d_out: bfloat16 [24, 1024, 768], P('dp', 'tp'), may hold values from -6 to 6
Outputs:
- output: bfloat16 [24, 1024, 768], P('dp', 'tp')
- d_tokens: float32 [24, 1024, 768], P('dp', 'tp')
- d_ln_gain: float32 [768], replicated
- d_qkv: float32 [768, 2304], P(None, 'tp')
- d_q_gain: float32 [12, 64], P('tp')
- d_k_gain: float32 [12, 64], P('tp')
- d_proj: float32 [768, 768], P('tp')
- d_fc1: float32 [768, 3072], P(None, 'tp')
- d_bias_one: float32 [3072], P('tp')
- d_fc2: float32 [3072, 768], P('tp')
- d_bias_two: float32 [768], replicated
Inputs may be any that keep to these rules, and one draw needn't show every extreme that they name: `lengths`: each image's length is one of 196, 576 and 1024; every draw holds all three.
All inputs are finite; a program needn't handle non-finite values.
Results may differ from a plain program's by a relative error of at most 0.014.
Values may be sent and summed in bfloat16 or wider, within the bound.
No kernel may reach another device: no remote copies, remote signals or barrier semaphores. Data moves between devices by JAX's collectives and lax.ppermute only.
A program may use at most 192 MiB of HBM per device.

v0:
```python
import jax
import jax.numpy as jnp
from jax import lax
from jax.sharding import PartitionSpec as P

epsilon = 1e-06
masked_value = -1e30


def layer_norm(values, scale_gain):
    average = jnp.mean(values, axis=-1, keepdims=True)
    centred = values - average
    variance = jnp.mean(centred * centred, axis=-1, keepdims=True)
    return centred * lax.rsqrt(variance + epsilon) * scale_gain


def gelu_exact(values):
    return jax.nn.gelu(values, approximate=False)


def score_block(queries, keys_normed, length, factor):
    scores = (
        jnp.einsum("qhd,khd->hqk", queries, keys_normed, preferred_element_type=jnp.float32)
        * factor
    )
    visible = lax.broadcasted_iota(jnp.int32, scores.shape, 2) < length
    return (scores, visible)


def forward_keys(factor, operands):
    queries, keys_normed, value_rows, length = operands
    scores, visible = score_block(queries, keys_normed, length, factor)
    masked = jnp.where(visible, scores, masked_value)
    row_peak = jnp.max(masked, axis=-1, keepdims=True)
    exponent = jnp.exp(masked - row_peak)
    row_total = jnp.sum(exponent, axis=-1, keepdims=True)
    probability = (exponent / row_total).astype(jnp.bfloat16)
    attended = jnp.einsum(
        "hqk,khd->qhd", probability, value_rows, preferred_element_type=jnp.float32
    )
    return (attended, row_peak[..., 0] + jnp.log(row_total[..., 0]))


def backward_keys(factor, operands):
    queries, keys_normed, value_rows, d_attended, logsum, length = operands
    scores, visible = score_block(queries, keys_normed, length, factor)
    probability = jnp.where(visible, jnp.exp(scores - logsum[..., None]), 0.0)
    d_probs = jnp.einsum("qhd,khd->hqk", d_attended, value_rows, preferred_element_type=jnp.float32)
    row_dot = jnp.sum(probability * d_probs, axis=-1, keepdims=True)
    d_scores = (probability * (d_probs - row_dot)).astype(jnp.bfloat16)
    d_queries = (
        jnp.einsum("hqk,khd->qhd", d_scores, keys_normed, preferred_element_type=jnp.float32)
        * factor
    )
    d_keys = (
        jnp.einsum("hqk,qhd->khd", d_scores, queries, preferred_element_type=jnp.float32) * factor
    )
    d_values = jnp.einsum(
        "hqk,qhd->khd",
        probability.astype(jnp.bfloat16),
        d_attended,
        preferred_element_type=jnp.float32,
    )
    return (d_queries, d_keys, d_values)


def shards(
    tokens, lengths, ln_gain, w_qkv, q_gain, k_gain, w_proj, w_fc1, b_fc1, w_fc2, b_fc2, d_out
):
    images = tokens.shape[0]
    heads_here = q_gain.shape[0]
    head_size = q_gain.shape[1]
    factor = head_size ** (-0.5)
    tokens_float = tokens.astype(jnp.float32)
    normed_local = layer_norm(tokens_float, ln_gain).astype(jnp.bfloat16)
    normed = lax.all_gather(normed_local, "tp", axis=1, tiled=True)
    seq_len = normed.shape[1]
    joined = jnp.einsum("bsd,dc->bsc", normed, w_qkv, preferred_element_type=jnp.float32)
    split_heads = joined.reshape(images, seq_len, heads_here, 3, head_size)
    query_raw = split_heads[:, :, :, 0]
    key_raw = split_heads[:, :, :, 1]
    queries = layer_norm(query_raw, q_gain).astype(jnp.bfloat16)
    keys_normed = layer_norm(key_raw, k_gain).astype(jnp.bfloat16)
    value_rows = split_heads[:, :, :, 2].astype(jnp.bfloat16)

    def attend_image(operands):
        return forward_keys(factor, operands)

    attended, logsum = lax.map(attend_image, (queries, keys_normed, value_rows, lengths))
    attended = attended.reshape(images, seq_len, heads_here * head_size).astype(jnp.bfloat16)
    hidden = jnp.einsum("bsd,df->bsf", normed, w_fc1, preferred_element_type=jnp.float32) + b_fc1
    active = gelu_exact(hidden).astype(jnp.bfloat16)
    partial_sum = jnp.einsum("bsc,cd->bsd", attended, w_proj, preferred_element_type=jnp.float32)
    partial_sum = partial_sum + jnp.einsum(
        "bsf,fd->bsd", active, w_fc2, preferred_element_type=jnp.float32
    )
    summed = lax.psum_scatter(
        partial_sum.astype(jnp.bfloat16), "tp", scatter_dimension=1, tiled=True
    ).astype(jnp.float32)
    output = (tokens_float + summed + b_fc2).astype(jnp.bfloat16)
    d_rows = lax.all_gather(d_out, "tp", axis=1, tiled=True)
    d_fc2 = jnp.einsum("bsf,bsd->fd", active, d_rows, preferred_element_type=jnp.float32)
    d_proj = jnp.einsum("bsc,bsd->cd", attended, d_rows, preferred_element_type=jnp.float32)
    d_active = jnp.einsum("bsd,fd->bsf", d_rows, w_fc2, preferred_element_type=jnp.float32)
    _, gelu_back = jax.vjp(gelu_exact, hidden)
    d_hidden = gelu_back(d_active)[0].astype(jnp.bfloat16)
    d_fc1 = jnp.einsum("bsd,bsf->df", normed, d_hidden, preferred_element_type=jnp.float32)
    d_bias_one = jnp.sum(d_hidden, axis=(0, 1), dtype=jnp.float32)
    d_normed = jnp.einsum("bsf,df->bsd", d_hidden, w_fc1, preferred_element_type=jnp.float32)
    d_attended = jnp.einsum(
        "bsd,cd->bsc", d_rows, w_proj, preferred_element_type=jnp.float32
    ).astype(jnp.bfloat16)
    d_heads = d_attended.reshape(images, seq_len, heads_here, head_size)

    def back_image(operands):
        return backward_keys(factor, operands)

    d_queries, d_keys, d_values = lax.map(
        back_image, (queries, keys_normed, value_rows, d_heads, logsum, lengths)
    )
    _, query_back = jax.vjp(layer_norm, query_raw, q_gain)
    d_query_raw, d_q_gain = query_back(d_queries)
    _, key_back = jax.vjp(layer_norm, key_raw, k_gain)
    d_key_raw, d_k_gain = key_back(d_keys)
    d_joined = (
        jnp.stack([d_query_raw, d_key_raw, d_values], axis=3)
        .reshape(images, seq_len, -1)
        .astype(jnp.bfloat16)
    )
    d_qkv = jnp.einsum("bsd,bsc->dc", normed, d_joined, preferred_element_type=jnp.float32)
    d_normed = d_normed + jnp.einsum(
        "bsc,dc->bsd", d_joined, w_qkv, preferred_element_type=jnp.float32
    )
    d_local = lax.psum_scatter(
        d_normed.astype(jnp.bfloat16), "tp", scatter_dimension=1, tiled=True
    ).astype(jnp.float32)
    _, norm_back = jax.vjp(layer_norm, tokens_float, ln_gain)
    d_tokens_part, d_ln_gain = norm_back(d_local)
    d_tokens = d_out.astype(jnp.float32) + d_tokens_part
    d_bias_two = jnp.sum(d_out, axis=(0, 1), dtype=jnp.float32)
    d_ln_gain, d_bias_two = lax.psum((d_ln_gain, d_bias_two), ("tp", "dp"))
    d_qkv, d_q_gain, d_k_gain, d_proj, d_fc1, d_bias_one, d_fc2 = (
        lax.psum(d_qkv.astype(jnp.bfloat16), "dp").astype(jnp.float32),
        lax.psum(d_q_gain.astype(jnp.bfloat16), "dp").astype(jnp.float32),
        lax.psum(d_k_gain.astype(jnp.bfloat16), "dp").astype(jnp.float32),
        lax.psum(d_proj.astype(jnp.bfloat16), "dp").astype(jnp.float32),
        lax.psum(d_fc1.astype(jnp.bfloat16), "dp").astype(jnp.float32),
        lax.psum(d_bias_one.astype(jnp.bfloat16), "dp").astype(jnp.float32),
        lax.psum(d_fc2.astype(jnp.bfloat16), "dp").astype(jnp.float32),
    )
    return (
        output,
        d_tokens,
        d_ln_gain,
        d_qkv,
        d_q_gain,
        d_k_gain,
        d_proj,
        d_fc1,
        d_bias_one,
        d_fc2,
        d_bias_two,
    )


def solution(mesh):
    placed = (
        P("dp", "tp", None),
        P("dp"),
        P(),
        P(None, "tp"),
        P("tp", None),
        P("tp", None),
        P("tp", None),
        P(None, "tp"),
        P("tp"),
        P("tp", None),
        P(),
        P("dp", "tp", None),
    )
    return jax.shard_map(
        shards,
        mesh=mesh,
        in_specs=placed,
        out_specs=(
            P("dp", "tp", None),
            P("dp", "tp", None),
            P(),
            P(None, "tp"),
            P("tp", None),
            P("tp", None),
            P("tp", None),
            P(None, "tp"),
            P("tp"),
            P("tp", None),
            P(),
        ),
        check_vma=False,
    )
```

profile of v0, /device:TPU:0, one launch (start us, length us, event | category | flops | bytes accessed | tf_op | source)
XLA Modules:
  0.0 569.2 jit_solution(9019446906122960374)
XLA Ops:
  17.7 36.0 %all-gather.3.cloned.1.call-done = bf16[3,1024,768]{2,1,0:T(8,128)(2,1)} async-done(((bf16[3,256,768]{2,1,0:T(8,128)(2,1)}), bf16[3,1024,768]{2,1,0:T(8,128)(2,1)}) %all-gather.3.cloned.1.call-update) | async-done | bytes 4718608 | tf_op jit(solution)/shard_map/all_gather | solution.py:76
  64.5 37.1 %while.28 = (s32[]{:T(128)}, bf16[3,1024,3,64]{1,3,2,0:T(8,128)(2,1)}, f32[3,3,1024]{2,1,0:T(4,128)}, bf16[3,1024,3,64]{1,3,2,0:T(8,128)(2,1)}, s32[3]{0:T(128)S...) while((s32[]{:T(128)}, bf16[3,1024,3,64]{1,3,2,0:T(8,128)(2,1)}, ...), condition=%wide.region_9.10_spmd.clone, body=%wide.region_6.9_spmd.sunk.clone | while | flops 843053056 | bytes 39823964 | solution.py:89
  101.6 6.0 %convolution_convert_fusion = bf16[3,1024,192]{1,2,0:T(8,128)(2,1)} fusion(bf16[3,1024,768]{2,1,0:T(8,128)(2,1)} %all-gather.5.cloned.1.call-done, bf16[192,768]{1,0:T(8,128)(2,1)} %param.22), kind=kOutput, calls=%fused_computation.126 | convolution fusion | flops 906559488 | bytes 6193152 | tf_op jit(solution)/shard_map/bsd,cd->bsc/dot_general | solution.py:110
  107.6 87.6 %while.29 = (s32[]{:T(128)}, f32[3,1024,3,64]{1,3,2,0:T(8,128)}, f32[3,1024,3,64]{1,3,2,0:T(8,128)}, bf16[3,1024,3,64]{1,3,2,0:T(8,128)(2,1)}, bf16[3,1024,3,64]...) while((s32[]{:T(128)}, f32[3,1024,3,64]{1,3,2,0:T(8,128)}, ...), condition=%wide.region_13.14_spmd.clone, body=%wide.region_11.13_spmd.sunk.clone | while | flops 2060843008 | bytes 124744848 | solution.py:118
  117.7 5.6 multiply_convert_fusion.6
  123.3 6.0 %fusion.164 = f32[3,1024,3,64]{1,3,2,0:T(8,128)} fusion(f32[3,1024,3,64]{1,3,2,0:T(8,128)} %get-tuple-element.364, s32[]{:T(128)} %get-tuple-element.362, bf16[3,1024,1024]{1,2,0:T(8,128)(2,1)} %multiply_convert_fusion.6, bf16[3,1024,3,64]{1,3,2,0:T(8,128)(2,1)} %get-tuple-element.378), kind=kOutput, calls=%fused_computation.31.clone.1.clone | convolution fusion | flops 402849792 | bytes 7472128 | tf_op jit(solution)/shard_map/while/body/eval_jaxpr/hqk,qhd->khd/dot_general | solution.py:56
  146.8 5.6 multiply_convert_fusion.6
  152.4 6.0 %fusion.164 = f32[3,1024,3,64]{1,3,2,0:T(8,128)} fusion(f32[3,1024,3,64]{1,3,2,0:T(8,128)} %get-tuple-element.364, s32[]{:T(128)} %get-tuple-element.362, bf16[3,1024,1024]{1,2,0:T(8,128)(2,1)} %multiply_convert_fusion.6, bf16[3,1024,3,64]{1,3,2,0:T(8,128)(2,1)} %get-tuple-element.378), kind=kOutput, calls=%fused_computation.31.clone.1.clone | convolution fusion | flops 402849792 | bytes 7472128 | tf_op jit(solution)/shard_map/while/body/eval_jaxpr/hqk,qhd->khd/dot_general | solution.py:56
  175.8 5.6 multiply_convert_fusion.6
  181.5 6.0 %fusion.164 = f32[3,1024,3,64]{1,3,2,0:T(8,128)} fusion(f32[3,1024,3,64]{1,3,2,0:T(8,128)} %get-tuple-element.364, s32[]{:T(128)} %get-tuple-element.362, bf16[3,1024,1024]{1,2,0:T(8,128)(2,1)} %multiply_convert_fusion.6, bf16[3,1024,3,64]{1,3,2,0:T(8,128)(2,1)} %get-tuple-element.378), kind=kOutput, calls=%fused_computation.31.clone.1.clone | convolution fusion | flops 402849792 | bytes 7472128 | tf_op jit(solution)/shard_map/while/body/eval_jaxpr/hqk,qhd->khd/dot_general | solution.py:56
  207.1 6.4 %fusion.72 = (u8[1024,768]{1,0:T(8,128)(4,1)S(1)}, u8[1024,768]{1,0:T(8,128)(4,1)S(1)}, f32[3,1024,768]{2,1,0:T(8,128)S(1)}) fusion(f32[768]{0:T(1024)S(1)} %copy-done.43, bf16[3,1024,768]{2,1,0:T(8,128)(2,1)S(1)} %bitcast.228, bf16[768,768]{1,0:T(8,128)(2,1)S(1)} %copy-done), kind=kOutput, calls=%fused_computation.122 | convolution fusion | flops 3655335936 | bytes 16911360 | tf_op jit(solution)/shard_map/bsd,df->bsf/dot_general | solution.py:91
  213.5 23.0 %multiply_convert_fusion.1 = (bf16[3,1024,768]{2,1,0:T(8,128)(2,1)S(1)}, f32[3,1024,768]{2,1,0:T(8,128)}) fusion(f32[3,1024,768]{2,1,0:T(8,128)S(1)} %get-tuple-element.172, f32[768]{0:T(1024)S(1)} %copy-done.43, u8[1024,768]{1,0:T(8,128)(4,1)S(1)} %get-tuple-element.109, u8[1024,768]{1,0:T(8,128)(4,1)S(1)} %get-tuple-element.108), kind=kLoop, calls=%fused_computation.70 | loop fusion | flops 167510016 | bytes 25168896 | tf_op jit(solution)/shard_map/convert_element_type | solution.py:92
  236.5 7.9 %bitcast_convert_fusion.2 = bf16[768,576]{0,1:T(8,128)(2,1)} fusion(bf16[3,1024,576]{1,2,0:T(8,128)(2,1)S(1)} %bitcast.224, bf16[3,1024,768]{2,1,0:T(8,128)(2,1)} %all-gather.3.cloned.1.call-done), kind=kOutput, calls=%fused_computation.125 | convolution fusion | flops 2718351360 | bytes 9142272 | tf_op jit(solution)/shard_map/bsd,bsc->dc/dot_general | solution.py:130
  249.0 14.2 %fusion.98 = (bf16[768]{0:T(1024)(128)(2,1)S(1)}, bf16[3,1024,768]{2,1,0:T(8,128)(2,1)}) fusion(f32[3,1024,768]{2,1,0:T(8,128)} %get-tuple-element.160, bf16[3,1024,768]{2,1,0:T(8,128)(2,1)} %all-gather.5.cloned.1.call-done, bf16[768,768]{1,0:T(8,128)(2,1)S(1)} %copy-done.44, f32[3,1024,768]{2,1,0:T(8,128)S(1)} %get-tuple-element.172, f32[768]{0:T(1024)S(1)} %copy-done.43), kind=kOutput, calls=%fused_computation.165 | convolution fusion | flops 3661626624 | bytes 29495808 | tf_op jit(solution)/shard_map/bsd,fd->bsf/dot_general | solution.py:104
  263.2 8.7 %bitcast_convert_fusion.1 = bf16[768,768]{1,0:T(8,128)(2,1)} fusion(bf16[3,1024,768]{2,1,0:T(8,128)(2,1)} %all-gather.3.cloned.1.call-done, bf16[3,1024,768]{2,1,0:T(8,128)(2,1)} %get-tuple-element.174), kind=kOutput, calls=%fused_computation.108 | convolution fusion | flops 3624468480 | bytes 10616832 | tf_op jit(solution)/shard_map/bsd,bsf->df/dot_general | solution.py:107
  271.9 7.3 %bitcast_convert_fusion = bf16[768,768]{1,0:T(8,128)(2,1)} fusion(bf16[3,1024,768]{2,1,0:T(8,128)(2,1)S(1)} %get-tuple-element.159, bf16[3,1024,768]{2,1,0:T(8,128)(2,1)} %all-gather.5.cloned.1.call-done), kind=kOutput, calls=%fused_computation.107 | convolution fusion | flops 3624468480 | bytes 10616832 | tf_op jit(solution)/shard_map/bsf,bsd->fd/dot_general | solution.py:102
  279.3 5.9 %fusion.81 = f32[3,1024,768]{2,1,0:T(8,128)S(1)} fusion(bf16[3,1024,768]{2,1,0:T(8,128)(2,1)} %get-tuple-element.174, bf16[768,768]{1,0:T(8,128)(2,1)S(1)} %copy-done), kind=kOutput, calls=%fused_computation.136 | convolution fusion | flops 3623878656 | bytes 15335424 | tf_op jit(solution)/shard_map/bsf,df->bsd/dot_general | solution.py:109
  285.3 5.6 add_convert_fusion
  291.0 6.1 %fusion.79 = f32[3,1024,768]{2,1,0:T(8,128)S(1)} fusion(bf16[3,1024,768]{2,1,0:T(8,128)(2,1)} %copy-done.13, bf16[768,768]{1,0:T(8,128)(2,1)S(1)} %copy-done.44), kind=kOutput, calls=%fused_computation.134 | convolution fusion | flops 3623878656 | bytes 15335424 | tf_op jit(solution)/shard_map/bsf,fd->bsd/dot_general | solution.py:94
  302.0 22.5 %all-reduce.1 = (bf16[3,64]{1,0:T(4,128)(2,1)S(1)}, bf16[3,64]{1,0:T(4,128)(2,1)S(1)}, bf16[768]{0:T(1024)(128)(2,1)S(1)}) all-reduce(bf16[3,64]{1,0:T(4,128)(2,1)S(1)} %get-tuple-element.176, bf16[3,64]{1,0:T(4,128)(2,1)S(1)} %get-tuple-element.110, bf16[768]{0:T(1024)(128)(2,1)S(1)} %get-tuple-element.173), channel_id=1, replica_groups=mesh['tp'=4,'dp'=8] {'dp'}, use_global_device_ids=true, to_apply=%region_25.26 | all-reduce | flops 1152 | bytes 4608 | tf_op jit(solution)/shard_map/psum | solution.py:144
  326.3 92.2 %all-reduce.5.cloned.1.call-done = (bf16[768,576]{0,1:T(8,128)(2,1)}, bf16[192,768]{1,0:T(8,128)(2,1)}, bf16[768,768]{1,0:T(8,128)(2,1)}, bf16[768,768]{1,0:T(8,128)(2,1)}) async-done(((bf16[768,576]{0,1:T(8,128)(2,1)}, bf16[192,768]{1,0:T(8,128)(2,1)}, bf16[768,768]{1,0:T(8,128)(2,1)}, bf16[768,768]{1,0:T(8,128)(2,1)}), (bf16[768,576]{0,1:T(8,128)(2,1)}, bf16[192,768]{1,0:T(8,128)(2,1)}, ...) | async-done | bytes 3538960 | tf_op jit(solution)/shard_map/psum | solution.py:143
  425.3 42.6 %reduce-scatter.5.cloned.1.call-done = bf16[3,256,768]{2,1,0:T(8,128)(2,1)} async-done(((bf16[3,1024,768]{2,1,0:T(8,128)(2,1)}), bf16[3,256,768]{2,1,0:T(8,128)(2,1)}) %reduce-scatter.5.cloned.1.call-update) | async-done | bytes 1179664 | tf_op jit(solution)/shard_map/reduce_scatter | solution.py:134
  473.1 45.0 %reduce-scatter.3.cloned.1.call-done = bf16[3,256,768]{2,1,0:T(8,128)(2,1)} async-done(((bf16[3,1024,768]{2,1,0:T(8,128)(2,1)}), bf16[3,256,768]{2,1,0:T(8,128)(2,1)}) %reduce-scatter.3.cloned.1.call-update) | async-done | bytes 1179664 | tf_op jit(solution)/shard_map/reduce_scatter | solution.py:97
  522.6 39.6 %all-reduce = (f32[768]{0:T(1024)}, f32[768]{0:T(1024)}) all-reduce(f32[768]{0:T(1024)} %get-tuple-element.114, f32[768]{0:T(1024)} %get-tuple-element.169), channel_id=1, replica_groups=mesh['tp'=4,'dp'=8] {'tp','dp'}, use_global_device_ids=true, to_apply=%region_22.23 | all-reduce | flops 1536 | bytes 12288 | tf_op jit(solution)/shard_map/psum | solution.py:141
  (203 shorter events, 150.2 us)
Async XLA Ops:
  7.2 199.6 %copy-start = (bf16[768,768]{1,0:T(8,128)(2,1)S(1)}, bf16[768,768]{1,0:T(8,128)(2,1)}, u32[]{:S(2)}) copy-start(bf16[768,768]{1,0:T(8,128)(2,1)} %param.23) | copy-start | bytes 3538948
  7.2 4.7 copy-start.6
  7.2 46.4 %all-gather.3.cloned.1.call-start = ((), (), s32[]{:S(2)}) async-start(), calls=%async_computation.2 | async-start | bytes 5898240 | tf_op jit(solution)/shard_map/all_gather | solution.py:76
  13.3 40.3 %copy-start.45 = (bf16[768,576]{0,1:T(8,128)(2,1)S(1)}, bf16[768,576]{0,1:T(8,128)(2,1)}, u32[]{:S(2)}) copy-start(bf16[768,576]{0,1:T(8,128)(2,1)} %param.19) | copy-start | bytes 2654212
  13.3 88.3 %all-gather.5.cloned.1.call-start = ((), (), s32[]{:S(2)}) async-start(), calls=%async_computation.4 | async-start | bytes 5898240 | tf_op jit(solution)/shard_map/all_gather | solution.py:101
  14.1 404.4 %all-reduce.5.cloned.1.call-start = ((), (), s32[]{:S(2)}) async-start(), calls=%async_computation.6 | async-start | bytes 7077888 | tf_op jit(solution)/shard_map/psum | solution.py:143
  101.6 6.0 %copy-start.8 = (bf16[3,1024,3,64]{1,3,2,0:T(8,128)(2,1)}, bf16[3,1024,3,64]{1,3,2,0:T(8,128)(2,1)S(1)}, u32[]{:S(2)}) copy-start(bf16[3,1024,3,64]{1,3,2,0:T(8,128)(2,1)S(1)} %get-tuple-element.394) | copy-start | bytes 3538948
  101.6 6.0 %copy-start.9 = (bf16[3,1024,3,64]{1,3,2,0:T(8,128)(2,1)}, bf16[3,1024,3,64]{1,3,2,0:T(8,128)(2,1)S(1)}, u32[]{:S(2)}) copy-start(bf16[3,1024,3,64]{1,3,2,0:T(8,128)(2,1)S(1)} %get-tuple-element.395) | copy-start | bytes 3538948
  107.6 87.6 %copy-start.5 = (f32[3,1024,3,1,64]{1,4,3,2,0:T(8,128)S(1)}, f32[3,1024,3,1,64]{1,4,3,2,0:T(8,128)}, u32[]{:S(2)}) copy-start(f32[3,1024,3,1,64]{1,4,3,2,0:T(8,128)} %copy-done.4) | copy-start | bytes 7077892
  107.6 87.6 %copy-start.40 = (f32[3,64]{1,0:T(4,128)S(1)}, f32[3,64]{1,0:T(4,128)}, u32[]{:S(2)}) copy-start(f32[3,64]{1,0:T(4,128)} %param.20) | copy-start | bytes 2308
  123.3 6.0 %copy-start.1 = (bf16[3,1024,1024]{1,2,0:T(8,128)(2,1)S(1)}, bf16[3,1024,1024]{1,2,0:T(8,128)(2,1)}, u32[]{:S(2)}) copy-start(bf16[3,1024,1024]{1,2,0:T(8,128)(2,1)} %multiply_convert_fusion.6) | copy-start | bytes 18874372 | tf_op jit(solution)/shard_map/while
  152.4 6.0 %copy-start.1 = (bf16[3,1024,1024]{1,2,0:T(8,128)(2,1)S(1)}, bf16[3,1024,1024]{1,2,0:T(8,128)(2,1)}, u32[]{:S(2)}) copy-start(bf16[3,1024,1024]{1,2,0:T(8,128)(2,1)} %multiply_convert_fusion.6) | copy-start | bytes 18874372 | tf_op jit(solution)/shard_map/while
  181.5 6.0 %copy-start.1 = (bf16[3,1024,1024]{1,2,0:T(8,128)(2,1)S(1)}, bf16[3,1024,1024]{1,2,0:T(8,128)(2,1)}, u32[]{:S(2)}) copy-start(bf16[3,1024,1024]{1,2,0:T(8,128)(2,1)} %multiply_convert_fusion.6) | copy-start | bytes 18874372 | tf_op jit(solution)/shard_map/while
  207.1 29.4 %copy-start.14 = (bf16[3,1024,3,3,64]{1,4,3,2,0:T(8,128)(2,1)}, bf16[3,1024,3,3,64]{1,4,3,2,0:T(8,128)(2,1)S(1)}, u32[]{:S(2)}) copy-start(bf16[3,1024,3,3,64]{1,4,3,2,0:T(8,128)(2,1)S(1)} %copy.30) | copy-start | bytes 10616836
  236.5 35.4 %copy-start.13 = (bf16[3,1024,768]{2,1,0:T(8,128)(2,1)}, bf16[3,1024,768]{2,1,0:T(8,128)(2,1)S(1)}, u32[]{:S(2)}) copy-start(bf16[3,1024,768]{2,1,0:T(8,128)(2,1)S(1)} %get-tuple-element.159) | copy-start | bytes 14155780
  279.2 6.0 %copy-start.46 = (bf16[768,576]{0,1:T(8,128)(2,1)S(1)}, bf16[768,576]{0,1:T(8,128)(2,1)}, u32[]{:S(2)}) copy-start(bf16[768,576]{0,1:T(8,128)(2,1)} %param.19) | copy-start | bytes 2654212
  279.3 188.6 %reduce-scatter.5.cloned.1.call-start = ((), (), s32[]{:S(2)}) async-start(), calls=%async_computation.5 | async-start | bytes 5898240 | tf_op jit(solution)/shard_map/reduce_scatter | solution.py:134
  279.3 6.0 %copy-start.15 = (bf16[3,1024,3,3,64]{1,4,3,2,0:T(8,128)(2,1)S(1)}, bf16[3,1024,3,3,64]{1,4,3,2,0:T(8,128)(2,1)}, u32[]{:S(2)}) copy-start(bf16[3,1024,3,3,64]{1,4,3,2,0:T(8,128)(2,1)} %copy-done.14) | copy-start | bytes 10616836
  290.9 6.1 %copy-start.31 = (bf16[192,768]{1,0:T(8,128)(2,1)S(1)}, bf16[192,768]{1,0:T(8,128)(2,1)}, u32[]{:S(2)}) copy-start(bf16[192,768]{1,0:T(8,128)(2,1)} %param.22) | copy-start | bytes 884740
  291.0 227.1 %reduce-scatter.3.cloned.1.call-start = ((), (), s32[]{:S(2)}) async-start(), calls=%async_computation.3 | async-start | bytes 5898240 | tf_op jit(solution)/shard_map/reduce_scatter | solution.py:97
  423.0 44.8 %copy-start.7 = (bf16[3,256,768]{2,1,0:T(8,128)(2,1)S(1)}, bf16[3,256,768]{2,1,0:T(8,128)(2,1)}, u32[]{:S(2)}) copy-start(bf16[3,256,768]{2,1,0:T(8,128)(2,1)} %param.16) | copy-start | bytes 3538948
  423.0 44.8 %copy-start.33 = (f32[3,256]{1,0:T(4,128)S(1)}, f32[3,256]{1,0:T(4,128)}, u32[]{:S(2)}) copy-start(f32[3,256]{1,0:T(4,128)} %copy-done.32) | copy-start | bytes 9220
  423.1 44.8 %copy-start.35 = (f32[768]{0:T(1024)S(1)}, f32[768]{0:T(1024)}, u32[]{:S(2)}) copy-start(f32[768]{0:T(1024)} %param.18) | copy-start | bytes 9220
  423.1 47.5 %copy-start.37 = (f32[3,256]{1,0:T(4,128)S(1)}, f32[3,256]{1,0:T(4,128)}, u32[]{:S(2)}) copy-start(f32[3,256]{1,0:T(4,128)} %copy-done.36) | copy-start | bytes 9220
  (33 other events, 70.5 us)
Sparse Core Ops, SparseCore 0:
  13.5 40.1 all-gather.2
  55.2 37.4 all-gather.4
  279.4 139.1 all-reduce.4
  420.9 46.8 reduce-scatter.4
  470.2 47.8 reduce-scatter.2
where the time goes:
time: 580 us; the launch traced here: 569 us
  waiting for transfers between devices  216 us (37%)
  matrix products  169 us (29%)
  other arithmetic  91.3 us (16%)
  blocking collectives  62.1 us (11%)
  local copies, waits for them, and re-layouts  15.1 us (3%)
  between operations  14.8 us (3%)
    psum x1, waiting for transfers between devices, shards(): lax.psum(d_qkv.astype(jnp.bfloat16), 'dp').astype(jnp.float32)  92.2 us
    reduce_scatter x1, waiting for transfers between devices, shards(): lax.psum_scatter(partial_sum.astype(jnp.bfloat16), 'tp', scatter_dimensio...  45 us
    reduce_scatter x1, waiting for transfers between devices, shards(): lax.psum_scatter(d_normed.astype(jnp.bfloat16), 'tp', scatter_dimension=1...  42.6 us
    psum x1, blocking collectives, shards(): d_ln_gain, d_bias_two = lax.psum((d_ln_gain, d_bias_two), ('tp', 'dp'))  39.6 us
    all_gather x1, waiting for transfers between devices, shards(): normed = lax.all_gather(normed_local, 'tp', axis=1, tiled=True)  36 us
    convert_element_type x1, other arithmetic, shards(): active = gelu_exact(hidden).astype(jnp.bfloat16)  23 us
    psum x1, blocking collectives, shards(): lax.psum(d_q_gain.astype(jnp.bfloat16), 'dp').astype(jnp.float32)  22.5 us
    dot_general x3, matrix products, backward_keys(): jnp.einsum('hqk,qhd->khd', d_scores, queries, preferred_element_type=jnp....  17.9 us
  transfers between devices with their start and end apart: 5, of which 4 were waited for; matrix products, arithmetic and copies ran while one was open for 15% of the time, Pallas kernels for 0%

commit v1 on v0

--- a/solution.py
+++ b/solution.py
@@ -140,7 +140,7 @@
     d_bias_two = jnp.sum(d_out, axis=(0, 1), dtype=jnp.float32)
     d_ln_gain, d_bias_two = lax.psum((d_ln_gain, d_bias_two), ("tp", "dp"))
     d_qkv, d_q_gain, d_k_gain, d_proj, d_fc1, d_bias_one, d_fc2 = (
-        lax.psum(d_qkv.astype(jnp.bfloat16), "dp").astype(jnp.float32),
+        jnp.sum(lax.all_gather(d_qkv.astype(jnp.bfloat16), "dp"), axis=0).astype(jnp.float32),
         lax.psum(d_q_gain.astype(jnp.bfloat16), "dp").astype(jnp.float32),
         lax.psum(d_k_gain.astype(jnp.bfloat16), "dp").astype(jnp.float32),
         lax.psum(d_proj.astype(jnp.bfloat16), "dp").astype(jnp.float32),

time: 580 us -> 618 us (1.066)
  waiting for transfers between devices: 216 us -> 248 us
  matrix products: 169 us -> 154 us
  other arithmetic: 91.3 us -> 103 us
    all_gather x0 -> x1, waiting for transfers between devices: none -> 63.2 us  [shards(): lax.all_gather(d_qkv.astype(jnp.bfloat16), 'dp')]
    psum x1, waiting for transfers between devices: 92.2 us -> 60.4 us  [shards(): lax.psum(d_proj.astype(jnp.bfloat16), 'dp').astype(jnp.float32)]
  transfers between devices with their start and end apart: 5 -> 6, of which waited for: 4 -> 5; matrix products, arithmetic and copies ran while one was open for 15% -> 16% of each run, Pallas kernels for 0% -> 0%
where the time goes in v1:
time: 618 us; the launch traced here: 607 us
  waiting for transfers between devices  248 us (40%)
  matrix products  154 us (25%)
  other arithmetic  103 us (17%)
  blocking collectives  65.7 us (11%)
  local copies, waits for them, and re-layouts  20.4 us (3%)
  between operations  15 us (2%)
    all_gather x1, waiting for transfers between devices, shards(): lax.all_gather(d_qkv.astype(jnp.bfloat16), 'dp')  63.2 us
    psum x1, waiting for transfers between devices, shards(): lax.psum(d_proj.astype(jnp.bfloat16), 'dp').astype(jnp.float32)  60.4 us
    reduce_scatter x1, waiting for transfers between devices, shards(): lax.psum_scatter(partial_sum.astype(jnp.bfloat16), 'tp', scatter_dimensio...  45 us
    psum x1, blocking collectives, shards(): d_ln_gain, d_bias_two = lax.psum((d_ln_gain, d_bias_two), ('tp', 'dp'))  44.2 us
    reduce_scatter x1, waiting for transfers between devices, shards(): lax.psum_scatter(d_normed.astype(jnp.bfloat16), 'tp', scatter_dimension=1...  42.8 us
    all_gather x1, waiting for transfers between devices, shards(): normed = lax.all_gather(normed_local, 'tp', axis=1, tiled=True)  36 us
    convert_element_type x1, other arithmetic, shards(): active = gelu_exact(hidden).astype(jnp.bfloat16)  23.1 us
    psum x1, blocking collectives, shards(): lax.psum(d_q_gain.astype(jnp.bfloat16), 'dp').astype(jnp.float32)  21.5 us
  transfers between devices with their start and end apart: 6, of which 5 were waited for; matrix products, arithmetic and copies ran while one was open for 16% of the time, Pallas kernels for 0%

profile of v1, /device:TPU:0, one launch (start us, length us, event | category | flops | bytes accessed | tf_op | source)
XLA Modules:
  0.0 607.3 jit_solution(15468550538051052797)
XLA Ops:
  18.4 36.0 %all-gather.5.cloned.1.call-done = bf16[3,1024,768]{2,1,0:T(8,128)(2,1)} async-done(((bf16[3,256,768]{2,1,0:T(8,128)(2,1)}), bf16[3,1024,768]{2,1,0:T(8,128)(2,1)}) %all-gather.5.cloned.1.call-update) | async-done | bytes 4718608 | tf_op jit(solution)/shard_map/all_gather | solution.py:76
  64.9 36.2 %while.28 = (s32[]{:T(128)}, bf16[3,1024,3,64]{1,3,2,0:T(8,128)(2,1)}, f32[3,3,1024]{2,1,0:T(4,128)}, bf16[3,1024,3,64]{1,3,2,0:T(8,128)(2,1)}, s32[3]{0:T(128)S...) while((s32[]{:T(128)}, bf16[3,1024,3,64]{1,3,2,0:T(8,128)(2,1)}, ...), condition=%wide.region_9.10_spmd.clone, body=%wide.region_6.9_spmd.sunk.clone | while | flops 843053056 | bytes 49268896 | solution.py:89
  101.1 5.9 convolution_convert_fusion
  107.1 87.5 %while.29 = (s32[]{:T(128)}, f32[3,1024,3,64]{1,3,2,0:T(8,128)}, f32[3,1024,3,64]{1,3,2,0:T(8,128)}, bf16[3,1024,3,64]{1,3,2,0:T(8,128)(2,1)}, bf16[3,1024,3,64]...) while((s32[]{:T(128)}, f32[3,1024,3,64]{1,3,2,0:T(8,128)}, ...), condition=%wide.region_13.14_spmd.clone, body=%wide.region_11.13_spmd.sunk.clone | while | flops 2060843008 | bytes 124744864 | solution.py:118
  121.7 5.6 multiply_convert_fusion.6
  127.3 6.0 fusion.164
  150.8 5.6 multiply_convert_fusion.6
  156.4 6.0 fusion.164
  179.8 5.6 multiply_convert_fusion.6
  185.5 6.0 fusion.164
  204.3 6.4 %fusion.72 = (u8[1024,768]{1,0:T(8,128)(4,1)S(1)}, u8[1024,768]{1,0:T(8,128)(4,1)S(1)}, f32[3,1024,768]{2,1,0:T(8,128)S(1)}) fusion(f32[768]{0:T(1024)S(1)} %copy-done.45, bf16[3,1024,768]{2,1,0:T(8,128)(2,1)S(1)} %bitcast.236, bf16[768,768]{1,0:T(8,128)(2,1)S(1)} %copy-done), kind=kOutput, calls=%fused_computation.123 | convolution fusion | flops 3655335936 | bytes 16911360 | tf_op jit(solution)/shard_map/bsd,df->bsf/dot_general | solution.py:91
  210.7 23.1 %multiply_convert_fusion.1 = (bf16[3,1024,768]{2,1,0:T(8,128)(2,1)S(1)}, f32[3,1024,768]{2,1,0:T(8,128)}) fusion(f32[3,1024,768]{2,1,0:T(8,128)S(1)} %get-tuple-element.171, f32[768]{0:T(1024)S(1)} %copy-done.45, u8[1024,768]{1,0:T(8,128)(4,1)S(1)} %get-tuple-element.109, u8[1024,768]{1,0:T(8,128)(4,1)S(1)} %get-tuple-element.108), kind=kLoop, calls=%fused_computation.70 | loop fusion | flops 167510016 | bytes 25168896 | tf_op jit(solution)/shard_map/convert_element_type | solution.py:92
  241.0 11.9 %fusion.98 = (bf16[768]{0:T(1024)(128)(2,1)S(1)}, bf16[3,1024,768]{2,1,0:T(8,128)(2,1)}) fusion(f32[3,1024,768]{2,1,0:T(8,128)} %get-tuple-element.159, bf16[3,1024,768]{2,1,0:T(8,128)(2,1)} %all-gather.7.cloned.1.call-done, bf16[768,768]{1,0:T(8,128)(2,1)} %param.25, f32[3,1024,768]{2,1,0:T(8,128)S(1)} %get-tuple-element.171, f32[768]{0:T(1024)S(1)} %copy-done.45), kind=kOutput, calls=%fused_computation.166 | convolution fusion | flops 3661626624 | bytes 29495808 | tf_op jit(solution)/shard_map/bsd,fd->bsf/dot_general | solution.py:104
  253.0 7.3 %bitcast_convert_fusion.1 = bf16[768,768]{1,0:T(8,128)(2,1)} fusion(bf16[3,1024,768]{2,1,0:T(8,128)(2,1)S(1)} %bitcast.238, bf16[3,1024,768]{2,1,0:T(8,128)(2,1)} %get-tuple-element.173), kind=kOutput, calls=%fused_computation.109 | convolution fusion | flops 3624468480 | bytes 10616832 | tf_op jit(solution)/shard_map/bsd,bsf->df/dot_general | solution.py:107
  270.1 5.6 add_convert_fusion
  275.8 6.2 %fusion.79 = f32[3,1024,768]{2,1,0:T(8,128)S(1)} fusion(bf16[3,1024,768]{2,1,0:T(8,128)(2,1)} %copy-done.14, bf16[768,768]{1,0:T(8,128)(2,1)} %param.25), kind=kOutput, calls=%fused_computation.135 | convolution fusion | flops 3623878656 | bytes 15335424 | tf_op jit(solution)/shard_map/bsf,fd->bsd/dot_general | solution.py:94
  286.1 7.3 %bitcast_convert_fusion.2 = bf16[768,576]{0,1:T(8,128)(2,1)} fusion(bf16[3,1024,576]{1,2,0:T(8,128)(2,1)} %bitcast.233, bf16[3,1024,768]{2,1,0:T(8,128)(2,1)} %all-gather.5.cloned.1.call-done), kind=kOutput, calls=%fused_computation.126 | convolution fusion | flops 2718351360 | bytes 9142272 | tf_op jit(solution)/shard_map/bsd,bsc->dc/dot_general | solution.py:130
  293.5 21.5 %all-reduce.1 = (bf16[3,64]{1,0:T(4,128)(2,1)S(1)}, bf16[3,64]{1,0:T(4,128)(2,1)S(1)}, bf16[768]{0:T(1024)(128)(2,1)S(1)}) all-reduce(bf16[3,64]{1,0:T(4,128)(2,1)S(1)} %get-tuple-element.175, bf16[3,64]{1,0:T(4,128)(2,1)S(1)} %get-tuple-element.110, bf16[768]{0:T(1024)(128)(2,1)S(1)} %get-tuple-element.172), channel_id=1, replica_groups=mesh['tp'=4,'dp'=8] {'dp'}, use_global_device_ids=true, to_apply=%region_25.26 | all-reduce | flops 1152 | bytes 4608 | tf_op jit(solution)/shard_map/psum | solution.py:144
  316.8 60.4 %all-reduce.5.cloned.1.call-done = (bf16[192,768]{1,0:T(8,128)(2,1)}, bf16[768,768]{1,0:T(8,128)(2,1)}, bf16[768,768]{1,0:T(8,128)(2,1)}) async-done(((bf16[192,768]{1,0:T(8,128)(2,1)}, bf16[768,768]{1,0:T(8,128)(2,1)}, bf16[768,768]{1,0:T(8,128)(2,1)}), (bf16[192,768]{1,0:T(8,128)(2,1)}, bf16[768,768]{1,0:T(8,128)(2,1)}, bf16[768,768]{1,0:T(8,128)(2,1)})) %all-reduce.5.cloned.1.call-update) | async-done | bytes 2654224 | tf_op jit(solution)/shard_map/psum | solution.py:146
  383.6 42.8 %reduce-scatter.5.cloned.1.call-done = bf16[3,256,768]{2,1,0:T(8,128)(2,1)} async-done(((bf16[3,1024,768]{2,1,0:T(8,128)(2,1)}), bf16[3,256,768]{2,1,0:T(8,128)(2,1)}) %reduce-scatter.5.cloned.1.call-update) | async-done | bytes 1179664 | tf_op jit(solution)/shard_map/reduce_scatter | solution.py:134
  431.6 45.0 %reduce-scatter.3.cloned.1.call-done = bf16[3,256,768]{2,1,0:T(8,128)(2,1)} async-done(((bf16[3,1024,768]{2,1,0:T(8,128)(2,1)}), bf16[3,256,768]{2,1,0:T(8,128)(2,1)}) %reduce-scatter.3.cloned.1.call-update) | async-done | bytes 1179664 | tf_op jit(solution)/shard_map/reduce_scatter | solution.py:97
  481.1 44.2 %all-reduce = (f32[768]{0:T(1024)}, f32[768]{0:T(1024)}) all-reduce(f32[768]{0:T(1024)} %get-tuple-element.114, f32[768]{0:T(1024)} %get-tuple-element.168), channel_id=1, replica_groups=mesh['tp'=4,'dp'=8] {'tp','dp'}, use_global_device_ids=true, to_apply=%region_22.23 | all-reduce | flops 1536 | bytes 12288 | tf_op jit(solution)/shard_map/psum | solution.py:141
  525.4 63.2 %all-gather.9.cloned.1.call-done = bf16[6144,576]{0,1:T(8,128)(2,1)} async-done(((bf16[768,576]{0,1:T(8,128)(2,1)}), bf16[6144,576]{0,1:T(8,128)(2,1)}) %all-gather.9.cloned.1.call-update) | async-done | bytes 7077904 | tf_op jit(solution)/shard_map/all_gather | solution.py:143
  588.5 5.3 copy.42
  (233 shorter events, 165.0 us)
Async XLA Ops:
  7.2 197.1 %copy-start = (bf16[768,768]{1,0:T(8,128)(2,1)S(1)}, bf16[768,768]{1,0:T(8,128)(2,1)}, u32[]{:S(2)}) copy-start(bf16[768,768]{1,0:T(8,128)(2,1)} %param.23) | copy-start | bytes 3538948
  7.2 47.1 %all-gather.5.cloned.1.call-start = ((), (), s32[]{:S(2)}) async-start(), calls=%async_computation.2 | async-start | bytes 5898240 | tf_op jit(solution)/shard_map/all_gather | solution.py:76
  14.0 40.3 %copy-start.46 = (bf16[768,576]{0,1:T(8,128)(2,1)S(1)}, bf16[768,576]{0,1:T(8,128)(2,1)}, u32[]{:S(2)}) copy-start(bf16[768,576]{0,1:T(8,128)(2,1)} %param.19) | copy-start | bytes 2654212
  14.0 87.1 %all-gather.7.cloned.1.call-start = ((), (), s32[]{:S(2)}) async-start(), calls=%async_computation.4 | async-start | bytes 5898240 | tf_op jit(solution)/shard_map/all_gather | solution.py:101
  14.8 362.4 %all-reduce.5.cloned.1.call-start = ((), (), s32[]{:S(2)}) async-start(), calls=%async_computation.7 | async-start | bytes 5308416 | tf_op jit(solution)/shard_map/psum | solution.py:146
  107.1 87.5 %copy-start.3 = (f32[3,1024,3,1,64]{1,4,3,2,0:T(8,128)S(1)}, f32[3,1024,3,1,64]{1,4,3,2,0:T(8,128)}, u32[]{:S(2)}) copy-start(f32[3,1024,3,1,64]{1,4,3,2,0:T(8,128)} %copy-done.2) | copy-start | bytes 7077892
  107.1 87.5 %copy-start.44 = (f32[3,64]{1,0:T(4,128)S(1)}, f32[3,64]{1,0:T(4,128)}, u32[]{:S(2)}) copy-start(f32[3,64]{1,0:T(4,128)} %param.20) | copy-start | bytes 2308
  127.3 6.0 copy-start.1
  156.4 6.0 copy-start.1
  185.5 6.0 copy-start.1
  202.5 31.3 %slice-start.4 = ((s8[4718592]{0:T(1024)(128)(4,1)}), s8[4194304]{0:T(1024)(128)(4,1)S(1)}, s32[]{:S(2)}) async-start(s8[4718592]{0:T(1024)(128)(4,1)} %bitcast.239), calls=%async_computation.12 | async-start | bytes 8388608
  204.3 29.5 %slice-start.5 = ((s8[4718592]{0:T(1024)(128)(4,1)}), s8[524288]{0:T(1024)(128)(4,1)S(1)}, s32[]{:S(2)}) async-start(s8[4718592]{0:T(1024)(128)(4,1)} %bitcast.239), calls=%async_computation.13 | async-start | bytes 1048576
  210.7 23.1 %copy-start.17 = (bf16[3,1024,3,64]{1,3,2,0:T(8,128)(2,1)S(1)}, bf16[3,1024,3,64]{1,3,2,0:T(8,128)(2,1)}, u32[]{:S(2)}) copy-start(bf16[3,1024,3,64]{1,3,2,0:T(8,128)(2,1)} %get-tuple-element.103) | copy-start | bytes 3538948
  236.0 16.9 %slice-start.2 = ((s8[4718592]{0:T(1024)(128)(4,1)}), s8[524288]{0:T(1024)(128)(4,1)S(1)}, s32[]{:S(2)}) async-start(s8[4718592]{0:T(1024)(128)(4,1)} %bitcast.237), calls=%async_computation.10 | async-start | bytes 1048576
  241.0 12.0 %slice-start.3 = ((s8[4718592]{0:T(1024)(128)(4,1)}), s8[4194304]{0:T(1024)(128)(4,1)S(1)}, s32[]{:S(2)}) async-start(s8[4718592]{0:T(1024)(128)(4,1)} %bitcast.237), calls=%async_computation.11 | async-start | bytes 8388608
  260.4 166.0 %reduce-scatter.5.cloned.1.call-start = ((), (), s32[]{:S(2)}) async-start(), calls=%async_computation.5 | async-start | bytes 5898240 | tf_op jit(solution)/shard_map/reduce_scatter | solution.py:134
  275.7 6.3 %copy-start.18 = (bf16[3,1024,3,64]{1,3,2,0:T(8,128)(2,1)S(1)}, bf16[3,1024,3,64]{1,3,2,0:T(8,128)(2,1)}, u32[]{:S(2)}) copy-start(bf16[3,1024,3,64]{1,3,2,0:T(8,128)(2,1)} %get-tuple-element.103) | copy-start | bytes 3538948
  275.8 6.3 %copy-start.34 = (bf16[192,768]{1,0:T(8,128)(2,1)S(1)}, bf16[192,768]{1,0:T(8,128)(2,1)}, u32[]{:S(2)}) copy-start(bf16[192,768]{1,0:T(8,128)(2,1)} %param.22) | copy-start | bytes 884740
  275.8 200.9 %reduce-scatter.3.cloned.1.call-start = ((), (), s32[]{:S(2)}) async-start(), calls=%async_computation.3 | async-start | bytes 5898240 | tf_op jit(solution)/shard_map/reduce_scatter | solution.py:97
  285.8 302.7 %all-gather.9.cloned.1.call-start = ((), (), s32[]{:S(2)}) async-start(), calls=%async_computation.6 | async-start | bytes 7962624 | tf_op jit(solution)/shard_map/all_gather | solution.py:143
  379.0 47.3 %copy-start.7 = (bf16[3,256,768]{2,1,0:T(8,128)(2,1)S(1)}, bf16[3,256,768]{2,1,0:T(8,128)(2,1)}, u32[]{:S(2)}) copy-start(bf16[3,256,768]{2,1,0:T(8,128)(2,1)} %param.16) | copy-start | bytes 3538948
  379.0 47.3 %copy-start.36 = (f32[3,256]{1,0:T(4,128)S(1)}, f32[3,256]{1,0:T(4,128)}, u32[]{:S(2)}) copy-start(f32[3,256]{1,0:T(4,128)} %copy-done.35) | copy-start | bytes 9220
  379.0 47.3 %copy-start.37 = (f32[768]{0:T(1024)S(1)}, f32[768]{0:T(1024)}, u32[]{:S(2)}) copy-start(f32[768]{0:T(1024)} %param.18) | copy-start | bytes 9220
  382.0 47.1 %copy-start.39 = (f32[3,256]{1,0:T(4,128)S(1)}, f32[3,256]{1,0:T(4,128)}, u32[]{:S(2)}) copy-start(f32[3,256]{1,0:T(4,128)} %copy-done.38) | copy-start | bytes 9220
  (45 other events, 123.9 us)
Sparse Core Ops, SparseCore 0:
  14.1 40.1 all-gather.4
  55.9 37.4 all-gather.6
  260.5 116.5 all-reduce.4
  379.5 46.8 reduce-scatter.4
  428.7 47.8 reduce-scatter.2
  479.2 109.2 all-gather.8
